TPU v7x, 32 devices: a whole 2x2x4 slice. The times are simulated.
32 devices in a mesh: dp: 2 (over x), ctx: 16 (over z, y, core).
Axes of the slice: x: 2, y: 2, z: 4, core: 2. Of those that a mesh axis runs over, the one named last changes fastest.
Arguments:
- features: bfloat16 [2, 2048, 1024], P('dp', 'ctx'), may hold values from -6 to 6
- gate_in: bfloat16 [2, 2048, 1024], P('dp', 'ctx'), may hold values from -6 to 6
- state_in: bfloat16 [2, 2048, 64], P('dp', 'ctx'), may hold values from -0.59765625 to 0.59765625
- state_out: bfloat16 [2, 2048, 64], P('dp', 'ctx'), may hold values from -0.59765625 to 0.59765625
- step_size: float32 [2, 8, 2048], P('dp', None, 'ctx'), may hold values from 0 to 4096
- decay_rate: float32 [8], replicated, may hold values from 0 to 1
- user_ids: int32 [2, 2048], P('dp', 'ctx'), may hold values from 0 to 3, never falling along the last dimension, each value on 1 to 1024 neighbouring positions
- norm_gain: bfloat16 [1024], replicated, may hold values from 0.099609375 to 1.8984375
- out_weight: bfloat16 [1024, 512], P(('dp', 'ctx')), may hold values from -0.1875 to 0.1875
- out_grad: bfloat16 [2, 2048, 512], P('dp', 'ctx'), may hold values from -6 to 6
Outputs:
- mixed: bfloat16 [2, 2048, 512], P('dp', 'ctx')
- feature_grad: bfloat16 [2, 2048, 1024], P('dp', 'ctx')
- weight_grad: float32 [1024, 512], P(('dp', 'ctx'))
Inputs may be any that keep to these rules, and one draw needn't show every extreme that they name: `user_ids`: each of the 4 users of a history holds consecutive events; ids never fall along a history, and one user holds exactly 1024 events.
All inputs are finite; a program needn't handle non-finite values.
Results may differ from a plain program's by a relative error of at most 0.019.
Values may be sent and summed in bfloat16 or wider, within the bound.
A program may use at most 64 MiB of HBM per device.

v0:
```python
import jax
import jax.numpy as jnp
from jax import lax
from jax.sharding import PartitionSpec as P

eps = 1e-05


def carried_in(value, axis, join, neutral, backward):
    count, mine = (lax.axis_size(axis), lax.axis_index(axis))
    pieces = jax.tree.map(lambda part: lax.all_gather(part, axis), value)
    if backward:
        pieces = jax.tree.map(lambda part: part[::-1], pieces)
        mine = count - 1 - mine
    running = jax.tree.map(
        lambda part, zero: jnp.full_like(part, 0) + jnp.asarray(zero, part.dtype), value, neutral
    )

    def step(position, running):
        longer = join(running, jax.tree.map(lambda part: part[position], pieces))
        return jax.tree.map(lambda new, old: jnp.where(position < mine, new, old), longer, running)

    return lax.fori_loop(0, count - 1, step, running)


def padded(x, sides, width):
    for axis, dim in sides:
        size, length = (lax.axis_size(axis), x.shape[dim])
        up = [(i, (i + 1) % size) for i in range(size - 1)]
        down = [(j, i) for i, j in up]
        last = lax.slice_in_dim(x, length - width, length, axis=dim)
        leading = lax.slice_in_dim(x, 0, width, axis=dim)
        before = lax.ppermute(last, axis, up)
        after = lax.ppermute(leading, axis, down)
        x = jnp.concatenate([before, x, after], axis=dim)
    return x


def carry_combine(earlier, following):
    gain_out = (earlier[0].astype(jnp.float32) * following[0].astype(jnp.float32)).astype(
        jnp.bfloat16
    )
    state_out = (
        following[0].astype(jnp.float32)[:, None, None] * earlier[1].astype(jnp.float32)
        + following[1].astype(jnp.float32)
    ).astype(jnp.bfloat16)
    return (gain_out, state_out)


def block_terms(values, keys_in, reads, logdec, user_row, before_user, after_user):
    row_count = values.shape[0]
    head_count = logdec.shape[0]
    cumulative = jnp.cumsum(logdec, axis=1)
    total_log = cumulative[:, -1]
    intersections = jnp.dot(reads, keys_in.T, preferred_element_type=jnp.float32)
    same_user = user_row[:, None] == user_row[None, :]
    spread = cumulative[:, :, None] - cumulative[:, None, :]
    doubled = 1.0 + jnp.eye(row_count, dtype=jnp.float32)
    weights = jnp.where(
        same_user[None], intersections[None] * doubled[None] * jnp.exp(-jnp.abs(spread)), 0.0
    ).astype(jnp.bfloat16)
    per_head = values.reshape(row_count, head_count, -1)
    inner = jnp.einsum("hts,shp->thp", weights, per_head, preferred_element_type=jnp.float32)
    tail_user = (user_row == user_row[-1]).astype(jnp.float32)
    head_user = (user_row == user_row[0]).astype(jnp.float32)
    fwd_scale = (jnp.exp(total_log[:, None] - cumulative) * tail_user[None]).T
    rev_scale = (jnp.exp(cumulative) * head_user[None]).T
    fwd_keys = (keys_in[:, None, :] * fwd_scale[:, :, None]).astype(jnp.bfloat16)
    rev_keys = (keys_in[:, None, :] * rev_scale[:, :, None]).astype(jnp.bfloat16)
    fwd_state = jnp.einsum(
        "shn,shp->hnp", fwd_keys, per_head, preferred_element_type=jnp.float32
    ).astype(jnp.bfloat16)
    rev_state = jnp.einsum(
        "shn,shp->hnp", rev_keys, per_head, preferred_element_type=jnp.float32
    ).astype(jnp.bfloat16)
    passing = jnp.exp(total_log)
    fwd_gain = (passing * (user_row[-1] == before_user).astype(jnp.float32)).astype(jnp.bfloat16)
    rev_gain = (passing * (user_row[0] == after_user).astype(jnp.float32)).astype(jnp.bfloat16)
    return (inner, cumulative, fwd_gain, fwd_state, rev_gain, rev_state)


def apply_carries(
    inner, reads, cumulative, user_row, before_user, after_user, from_before, from_after
):
    earlier_part = jnp.einsum("tn,hnp->thp", reads, from_before, preferred_element_type=jnp.float32)
    following_part = jnp.einsum(
        "tn,hnp->thp", reads, from_after, preferred_element_type=jnp.float32
    )
    earlier_scale = (jnp.exp(cumulative) * (user_row == before_user).astype(jnp.float32)[None]).T[
        :, :, None
    ]
    following_scale = (
        jnp.exp(cumulative[:, -1:] - cumulative)
        * (user_row == after_user).astype(jnp.float32)[None]
    ).T[:, :, None]
    row_count = inner.shape[0]
    return (inner + earlier_scale * earlier_part + following_scale * following_part).reshape(
        row_count, -1
    )


def mix_local(values, keys_in, reads, logdec, user_row, before_user, after_user):
    inner, cumulative, fwd_gain, fwd_state, rev_gain, rev_state = block_terms(
        values, keys_in, reads, logdec, user_row, before_user, after_user
    )
    neutral = jnp.ones_like(fwd_gain)
    nothing = jnp.zeros_like(fwd_state)
    from_before = carried_in(
        (fwd_gain, fwd_state), "ctx", carry_combine, (neutral, nothing), False
    )[1]
    from_after = carried_in((rev_gain, rev_state), "ctx", carry_combine, (neutral, nothing), True)[
        1
    ]
    return apply_carries(
        inner, reads, cumulative, user_row, before_user, after_user, from_before, from_after
    )


def local(
    features,
    gate_in,
    state_in,
    state_out,
    step_size,
    decay_rate,
    user_ids,
    norm_gain,
    out_weight,
    out_grad,
):
    neighbours = padded(user_ids + 1, (("ctx", 1),), 1) - 1
    user_row = user_ids[0]
    before_user = neighbours[0, 0]
    after_user = neighbours[0, -1]
    logdec = -step_size[0] * decay_rate[:, None]
    values = features[0]
    gates = gate_in[0]
    keys_in = state_in[0]
    reads = state_out[0]
    grad_local = out_grad[0]
    mixed_wide = mix_local(values, keys_in, reads, logdec, user_row, before_user, after_user)

    def normalize(mixed_rows):
        gated = mixed_rows * jax.nn.silu(gates.astype(jnp.float32))
        multiplier_value = lax.rsqrt(jnp.mean(gated * gated, axis=-1, keepdims=True) + eps)
        return gated * multiplier_value * norm_gain.astype(jnp.float32)

    normed_wide, pullback = jax.vjp(normalize, mixed_wide)
    normed_out = normed_wide.astype(jnp.bfloat16)
    full_weight = lax.all_gather(out_weight, ("dp", "ctx"), axis=0, tiled=True)
    result = jnp.dot(normed_out, full_weight, preferred_element_type=jnp.float32)
    grad_normed = lax.dot_general(
        grad_local, full_weight, (((1,), (1,)), ((), ())), preferred_element_type=jnp.float32
    )
    grad_mixed = pullback(grad_normed)[0].astype(jnp.bfloat16)
    grad_feat = mix_local(grad_mixed, reads, keys_in, logdec, user_row, before_user, after_user)
    weight_grad = lax.psum_scatter(
        lax.dot_general(
            normed_out, grad_local, (((0,), (0,)), ((), ())), preferred_element_type=jnp.float32
        ),
        ("dp", "ctx"),
        scatter_dimension=0,
        tiled=True,
    )
    return (result.astype(jnp.bfloat16)[None], grad_feat.astype(jnp.bfloat16)[None], weight_grad)


def solution(mesh):
    placed = (
        P("dp", "ctx", None),
        P("dp", "ctx", None),
        P("dp", "ctx", None),
        P("dp", "ctx", None),
        P("dp", None, "ctx"),
        P(),
        P("dp", "ctx"),
        P(),
        P(("dp", "ctx"), None),
        P("dp", "ctx", None),
    )
    return jax.shard_map(
        local,
        mesh=mesh,
        in_specs=placed,
        out_specs=(P("dp", "ctx", None), P("dp", "ctx", None), P(("dp", "ctx"), None)),
        check_vma=False,
    )
```

profile of v0, /device:TPU:0, one launch (start us, length us, event | category | flops | bytes accessed | tf_op | source)
XLA Modules:
  0.0 400.2 jit_solution(13853915928123735821)
XLA Ops:
  8.6 2.9 collective-permute-start
  11.5 1.3 collective-permute-start.1
  12.7 1.3 fusion.76
  17.1 1.3 add_add_fusion.1
  19.0 3.2 fusion.67
  25.5 1.6 convolution_multiply_fusion.2
  27.1 1.3 bitcast_convert_fusion.5
  28.4 1.4 broadcast_compare_fusion
  35.0 36.1 %all-reduce.2 = (bf16[128]{0:T(256)(128)(2,1)S(1)}, bf16[128]{0:T(256)(128)(2,1)S(1)}) all-reduce(bf16[128]{0:T(256)(128)(2,1)S(1)} %dynamic-update-slice.1, bf16[128]{0:T(256)(128)(2,1)S(1)} %dynamic-update-slice), channel_id=4, replica_groups=mesh['dp'=2,'ctx'=16] {'ctx'}, use_global_device_ids=true, to_apply=%add.1 | all-reduce | flops 256 | bytes 1024
  72.4 1.8 rev.11
  74.3 29.6 %while.57 = (s32[]{:T(128)}, bf16[8,64,128]{2,1,0:T(8,128)(2,1)S(1)}, s32[]{:T(128)}, bf16[16,8]{1,0:T(8,128)(2,1)}, bf16[16,8,64,128]{3,2,1,0:T(8,128)(2,1)S(1)}, /*index=5*/s32[]{:T(128)}, s32[]{:T(128)}) while((s32[]{:T(128)}, bf16[8,64,128]{2,1,0:T(8,128)(2,1)S(1)}, s32[]{:T(128)}, bf16[16,8]{1,0:T(8,128)(2,1)}, ...), condition=%wide.region_4.5_spmd.clone, body=%wide.region_3.4_spmd.clone.sunk | while | flops 458764 | bytes 393401 | solution.py:23
  74.3 1.2 bitcast_convert_fusion.11
  76.2 1.2 bitcast_convert_fusion.11
  78.2 1.2 bitcast_convert_fusion.11
  80.2 1.2 bitcast_convert_fusion.11
  82.1 1.2 bitcast_convert_fusion.11
  84.1 1.2 bitcast_convert_fusion.11
  86.0 1.2 bitcast_convert_fusion.11
  88.0 1.2 bitcast_convert_fusion.11
  89.9 1.2 bitcast_convert_fusion.11
  91.9 1.2 bitcast_convert_fusion.11
  93.9 1.2 bitcast_convert_fusion.11
  95.9 1.2 bitcast_convert_fusion.11
  97.9 1.2 bitcast_convert_fusion.11
  99.9 1.2 bitcast_convert_fusion.11
  101.9 1.2 bitcast_convert_fusion.11
  103.9 8.7 %all-gather.14.cloned.1.call-done = bf16[128,64,128]{2,1,0:T(8,128)(2,1)} async-done(((bf16[8,64,128]{2,1,0:T(8,128)(2,1)}), bf16[128,64,128]{2,1,0:T(8,128)(2,1)}) %all-gather.14.cloned.1.call-update) | async-done | bytes 2097168 | tf_op jit(solution)/shard_map/all_gather | solution.py:11
  112.6 25.8 %while.56 = (s32[]{:T(128)}, bf16[8,64,128]{2,1,0:T(8,128)(2,1)S(1)}, s32[]{:T(128)}, bf16[16,8]{1,0:T(8,128)(2,1)}, bf16[16,8,64,128]{3,2,1,0:T(8,128)(2,1)}, /*index=5*/s32[]{:T(128)}, s32[]{:T(128)}) while((s32[]{:T(128)}, bf16[8,64,128]{2,1,0:T(8,128)(2,1)S(1)}, s32[]{:T(128)}, bf16[16,8]{1,0:T(8,128)(2,1)}, ...), condition=%wide.region_2.3_spmd.clone, body=%wide.region_1.2_spmd.clone.sunk | while | flops 458764 | bytes 393401 | solution.py:23
  113.2 1.0 fusion.89
  115.0 1.0 fusion.89
  116.7 1.0 fusion.89
  118.4 1.0 fusion.89
  120.1 1.0 fusion.89
  121.8 1.0 fusion.89
  123.5 1.0 fusion.89
  125.3 1.0 fusion.89
  127.0 1.0 fusion.89
  128.7 1.0 fusion.89
  130.4 1.0 fusion.89
  132.2 1.0 fusion.89
  133.9 1.0 fusion.89
  135.6 1.0 fusion.89
  137.3 1.0 fusion.89
  139.7 28.3 %all-gather.12.cloned.1.call-done = bf16[1024,512]{1,0:T(8,128)(2,1)} async-done(((bf16[32,512]{1,0:T(8,128)(2,1)}), bf16[1024,512]{1,0:T(8,128)(2,1)}) %all-gather.12.cloned.1.call-update) | async-done | bytes 1048592 | tf_op jit(solution)/shard_map/all_gather | solution.py:150
  168.0 1.8 multiply_reduce_fusion
  173.1 1.7 fusion.45
  174.8 2.3 fusion.17
  177.1 34.5 %all-gather.20.cloned.1.call-done = bf16[128,64,128]{2,1,0:T(8,128)(2,1)} async-done(((bf16[8,64,128]{2,1,0:T(8,128)(2,1)}), bf16[128,64,128]{2,1,0:T(8,128)(2,1)}) %all-gather.20.cloned.1.call-update) | async-done | bytes 2097168 | tf_op jit(solution)/shard_map/all_gather | solution.py:11
  211.6 1.8 rev.12
  213.4 12.1 %while.59 = (s32[]{:T(128)}, bf16[8,64,128]{2,1,0:T(8,128)(2,1)S(1)}, s32[]{:T(128)}, bf16[16,8]{1,0:T(8,128)(2,1)}, bf16[16,8,64,128]{3,2,1,0:T(8,128)(2,1)S(1)}, /*index=5*/s32[]{:T(128)}, s32[]{:T(128)}) while((s32[]{:T(128)}, bf16[8,64,128]{2,1,0:T(8,128)(2,1)S(1)}, s32[]{:T(128)}, bf16[16,8]{1,0:T(8,128)(2,1)}, ...), condition=%wide.region_10.11_spmd.clone, body=%wide.region_9.10_spmd.clone.sunk | while | flops 458764 | bytes 393401 | solution.py:23
  225.9 28.0 %all-gather.18.cloned.1.call-done = bf16[128,64,128]{2,1,0:T(8,128)(2,1)} async-done(((bf16[8,64,128]{2,1,0:T(8,128)(2,1)}), bf16[128,64,128]{2,1,0:T(8,128)(2,1)}) %all-gather.18.cloned.1.call-update) | async-done | bytes 2097168 | tf_op jit(solution)/shard_map/all_gather | solution.py:11
  253.9 25.8 %while.58 = (s32[]{:T(128)}, bf16[8,64,128]{2,1,0:T(8,128)(2,1)S(1)}, s32[]{:T(128)}, bf16[16,8]{1,0:T(8,128)(2,1)}, bf16[16,8,64,128]{3,2,1,0:T(8,128)(2,1)}, /*index=5*/s32[]{:T(128)}, s32[]{:T(128)}) while((s32[]{:T(128)}, bf16[8,64,128]{2,1,0:T(8,128)(2,1)S(1)}, s32[]{:T(128)}, bf16[16,8]{1,0:T(8,128)(2,1)}, ...), condition=%wide.region_8.9_spmd.clone, body=%wide.region_7.8_spmd.clone.sunk | while | flops 458764 | bytes 393401 | solution.py:23
  254.6 1.0 fusion.91
  256.3 1.0 fusion.91
  258.0 1.0 fusion.91
  261.4 1.0 fusion.91
  266.6 1.0 fusion.91
  268.3 1.0 fusion.91
  270.0 1.0 fusion.91
  273.5 1.0 fusion.91
  275.2 1.0 fusion.91
  276.9 1.0 fusion.91
  278.7 1.0 fusion.91
  281.3 112.0 %reduce-scatter.2.cloned.1.call-done = f32[32,512]{1,0:T(8,128)} async-done(((f32[1024,512]{1,0:T(8,128)}), f32[32,512]{1,0:T(8,128)}) %reduce-scatter.2.cloned.1.call-update) | async-done | bytes 65552 | tf_op jit(solution)/shard_map/reduce_scatter | solution.py:157
  (184 shorter events, 65.8 us)
Async XLA Ops:
  7.2 160.8 %copy-start = (bf16[1,128,512]{2,1,0:T(8,128)(2,1)S(1)}, bf16[1,128,512]{2,1,0:T(8,128)(2,1)}, u32[]{:S(2)}) copy-start(bf16[1,128,512]{2,1,0:T(8,128)(2,1)} %param.27) | copy-start | bytes 393220
  7.2 23.4 %copy-start.24 = (u32[32]{0:T(128)S(1)}, u32[32]{0:T(128)}, u32[]{:S(2)}) copy-start(u32[32]{0:T(128)} %constant.130) | copy-start | bytes 388
  7.2 22.6 %copy-start.1 = (bf16[1,128,1024]{2,1,0:T(8,128)(2,1)S(1)}, bf16[1,128,1024]{2,1,0:T(8,128)(2,1)}, u32[]{:S(2)}) copy-start(bf16[1,128,1024]{2,1,0:T(8,128)(2,1)} %param.19) | copy-start | bytes 786436
  7.2 22.8 %copy-start.23 = (bf16[1024]{0:T(1024)(128)(2,1)S(1)}, bf16[1024]{0:T(1024)(128)(2,1)}, u32[]{:S(2)}) copy-start(bf16[1024]{0:T(1024)(128)(2,1)} %param.25) | copy-start | bytes 6148
  7.2 65.2 %all-gather.16.cloned.1.call-start = ((), (), s32[]{:S(2)}) async-start(), calls=%async_computation.4 | async-start | bytes 2228224 | tf_op jit(solution)/shard_map/all_gather | solution.py:11
  8.6 8.5 %collective-permute-start = (s32[1,1]{1,0:T(1,128)}, s32[1,1]{1,0:T(1,128)}, u32[]{:S(2)}, u32[]{:S(2)}) collective-permute-start(s32[1,1]{1,0:T(1,128)} %get-tuple-element.528), channel_id=1, source_target_pairs={{0,1},{1,2},{2,3},{3,4},{4,5},{5,6},{6,7},{7,8},{8,9},{9,10},{10,1... | collective-permute-start | bytes 20 | tf_op jit(solution)/shard_map/ppermute | solution.py:33
  11.5 5.6 %collective-permute-start.1 = (s32[1,1]{1,0:T(1,128)}, s32[1,1]{1,0:T(1,128)}, u32[]{:S(2)}, u32[]{:S(2)}) collective-permute-start(s32[1,1]{1,0:T(1,128)} %get-tuple-element.529), channel_id=1, source_target_pairs={{1,0},{2,1},{3,2},{4,3},{5,4},{6,5},{7,6},{8,7},{9,8},{10,9},{11,1... | collective-permute-start | bytes 20 | tf_op jit(solution)/shard_map/ppermute | solution.py:34
  15.1 57.3 %copy-start.7 = (f32[8,128]{1,0:T(8,128)}, f32[8,128]{1,0:T(8,128)S(1)}, u32[]{:S(2)}) copy-start(f32[8,128]{1,0:T(8,128)S(1)} %reduce_window_sum.12) | copy-start | bytes 12292
  22.9 2.6 copy-start.17
  22.9 2.6 copy-start.19
  23.8 88.8 %all-gather.14.cloned.1.call-start = ((), (), s32[]{:S(2)}) async-start(), calls=%async_computation.3 | async-start | bytes 2228224 | tf_op jit(solution)/shard_map/all_gather | solution.py:11
  24.7 143.2 %all-gather.12.cloned.1.call-start = ((), (), s32[]{:S(2)}) async-start(), calls=%async_computation.1 | async-start | bytes 1081344 | tf_op jit(solution)/shard_map/all_gather | solution.py:150
  25.4 186.1 %all-gather.20.cloned.1.call-start = ((), (), s32[]{:S(2)}) async-start(), calls=%async_computation.6 | async-start | bytes 2228224 | tf_op jit(solution)/shard_map/all_gather | solution.py:11
  74.3 64.1 %copy-start.2 = (bf16[1,128,64]{1,2,0:T(8,128)(2,1)S(1)}, bf16[1,128,64]{1,2,0:T(8,128)(2,1)}, u32[]{:S(2)}) copy-start(bf16[1,128,64]{1,2,0:T(8,128)(2,1)} %param.21) | copy-start | bytes 49156
  103.8 34.6 %copy-start.15 = (f32[128,8]{0,1:T(8,128)S(1)}, f32[128,8]{0,1:T(8,128)}, u32[]{:S(2)}) copy-start(f32[128,8]{0,1:T(8,128)} %get-tuple-element.514) | copy-start | bytes 12292
  103.9 34.8 %copy-start.13 = (f32[128,8]{0,1:T(8,128)S(1)}, f32[128,8]{0,1:T(8,128)}, u32[]{:S(2)}) copy-start(f32[128,8]{0,1:T(8,128)} %get-tuple-element.512) | copy-start | bytes 12292
  103.9 35.1 %copy-start.8 = (f32[8,128]{1,0:T(8,128)S(1)}, f32[8,128]{1,0:T(8,128)}, u32[]{:S(2)}) copy-start(f32[8,128]{1,0:T(8,128)} %copy-done.7) | copy-start | bytes 12292
  103.9 35.1 %copy-start.10 = (pred[128,128]{1,0:T(8,128)(4,1)S(1)}, pred[128,128]{1,0:T(8,128)(4,1)}, u32[]{:S(2)}) copy-start(pred[128,128]{1,0:T(8,128)(4,1)} %broadcast_compare_fusion) | copy-start | bytes 49156
  103.9 35.1 %copy-start.12 = (f32[128,128]{1,0:T(8,128)S(1)}, f32[128,128]{1,0:T(8,128)}, u32[]{:S(2)}) copy-start(f32[128,128]{1,0:T(8,128)} %convolution_multiply_fusion.2) | copy-start | bytes 196612
  139.0 29.0 %copy-start.22 = (f32[1024]{0:T(1024)S(1)}, f32[1024]{0:T(1024)}, u32[]{:S(2)}) copy-start(f32[1024]{0:T(1024)} %get-tuple-element.517) | copy-start | bytes 12292
  168.0 2.1 copy-start.5
  168.0 2.1 copy-start.20
  168.0 3.1 copy-start.18
  169.8 2.3 copy-start.3
  169.8 3.1 copy-start.21
  171.0 82.9 %all-gather.18.cloned.1.call-start = ((), (), s32[]{:S(2)}) async-start(), calls=%async_computation.5 | async-start | bytes 2228224 | tf_op jit(solution)/shard_map/all_gather | solution.py:11
  172.0 221.4 %reduce-scatter.2.cloned.1.call-start = ((), (), s32[]{:S(2)}) async-start(), calls=%async_computation.2 | async-start | bytes 2162688 | tf_op jit(solution)/shard_map/reduce_scatter | solution.py:157
  213.4 12.2 %copy-start.4 = (bf16[1,128,64]{1,2,0:T(8,128)(2,1)S(1)}, bf16[1,128,64]{1,2,0:T(8,128)(2,1)}, u32[]{:S(2)}) copy-start(bf16[1,128,64]{1,2,0:T(8,128)(2,1)} %param.20) | copy-start | bytes 49156
  213.4 12.2 %copy-start.16 = (f32[128,8]{0,1:T(8,128)S(1)}, f32[128,8]{0,1:T(8,128)}, u32[]{:S(2)}) copy-start(f32[128,8]{0,1:T(8,128)} %get-tuple-element.514) | copy-start | bytes 12292
  213.4 66.3 %copy-start.14 = (f32[128,8]{0,1:T(8,128)S(1)}, f32[128,8]{0,1:T(8,128)}, u32[]{:S(2)}) copy-start(f32[128,8]{0,1:T(8,128)} %get-tuple-element.512) | copy-start | bytes 12292
  225.6 54.4 %copy-start.6 = (f32[128,128]{1,0:T(8,128)S(1)}, f32[128,128]{1,0:T(8,128)}, u32[]{:S(2)}) copy-start(f32[128,128]{1,0:T(8,128)} %convolution_multiply_fusion.1) | copy-start | bytes 196612
  225.6 54.4 %copy-start.9 = (f32[8,128]{1,0:T(8,128)S(1)}, f32[8,128]{1,0:T(8,128)}, u32[]{:S(2)}) copy-start(f32[8,128]{1,0:T(8,128)} %copy-done.7) | copy-start | bytes 12292
  225.6 54.4 %copy-start.11 = (pred[128,128]{1,0:T(8,128)(4,1)S(1)}, pred[128,128]{1,0:T(8,128)(4,1)}, u32[]{:S(2)}) copy-start(pred[128,128]{1,0:T(8,128)(4,1)} %broadcast_compare_fusion) | copy-start | bytes 49156
Sparse Core Ops, SparseCore 0:
  23.9 45.7 all-gather.15
  72.4 40.1 all-gather.13
  115.5 52.4 all-gather.11
  171.1 40.4 all-gather.19
  213.6 40.2 all-gather.17
  256.6 136.7 reduce-scatter.1
where the time goes:
time: 403 us; the launch traced here: 400 us
  waiting for transfers between devices  212 us (53%)
  other arithmetic  104 us (26%)
  blocking collectives  36.1 us (9%)
  between operations  17.7 us (4%)
  matrix products  13.7 us (3%)
  local copies, waits for them, and re-layouts  11.1 us (3%)
  starting transfers between devices  4.41 us (1%)
    reduce_scatter x1, waiting for transfers between devices, local(): lax.psum_scatter(lax.dot_general(normed_out, grad_local, (((0,), (0,)), (...  112 us
    all_gather x4, waiting for transfers between devices, carried_in(): pieces = jax.tree.map(lambda part: lax.all_gather(part, axis), value)  71.2 us
    convert_element_type x60, other arithmetic, carry_combine(): following[0].astype(jnp.float32)[:, None, None]  47.6 us
    select_n x60, other arithmetic, step(): jnp.where(position < mine, new, old)  44.8 us
    unnamed x1, blocking collectives  36.1 us
    all_gather x1, waiting for transfers between devices, local(): full_weight = lax.all_gather(out_weight, ('dp', 'ctx'), axis=0, tiled=True)  28.3 us
  transfers between devices with their start and end apart: 8, of which 5 were waited for; matrix products, arithmetic and copies ran while one was open for 29% of the time, Pallas kernels for 0%

commit v1 on v0

--- a/solution.py
+++ b/solution.py
@@ -6,21 +6,54 @@
 eps = 1e-05
 
 
-def carried_in(value, axis, join, neutral, backward):
-    count, mine = (lax.axis_size(axis), lax.axis_index(axis))
-    pieces = jax.tree.map(lambda part: lax.all_gather(part, axis), value)
-    if backward:
-        pieces = jax.tree.map(lambda part: part[::-1], pieces)
-        mine = count - 1 - mine
-    running = jax.tree.map(
-        lambda part, zero: jnp.full_like(part, 0) + jnp.asarray(zero, part.dtype), value, neutral
-    )
-
-    def step(position, running):
-        longer = join(running, jax.tree.map(lambda part: part[position], pieces))
-        return jax.tree.map(lambda new, old: jnp.where(position < mine, new, old), longer, running)
-
-    return lax.fori_loop(0, count - 1, step, running)
+def carried_in(gain, state, axis, backward):
+    count = lax.axis_size(axis)
+    window = count // 2
+    sign = -1 if backward else 1
+
+    def shifted(value, distance):
+        pairs = [
+            (i, i + sign * distance) for i in range(count) if 0 <= i + sign * distance < count
+        ]
+        return lax.ppermute(value, axis, pairs)
+
+    heads, _, width = state.shape
+    distance = 1
+    while distance < window:
+        row = jnp.broadcast_to(gain[:, None, None], (heads, 8, width))
+        far = shifted(jnp.concatenate([state, row], axis=1), distance)
+        wide = gain.astype(jnp.float32)
+        state = (
+            wide[:, None, None] * far[:, :-8].astype(jnp.float32) + state.astype(jnp.float32)
+        ).astype(jnp.bfloat16)
+        gain = (wide * far[:, -1, 0].astype(jnp.float32)).astype(jnp.bfloat16)
+        distance *= 2
+    return shifted(state, 1)
+
+
+def summed_rows(partial, axes):
+    sizes = [lax.axis_size(axis) for axis in axes]
+    total = 1
+    for size in sizes:
+        total *= size
+    mine = lax.axis_index(axes)
+    bits = []
+    bit = 1
+    while bit < total:
+        bits.append(bit)
+        bit *= 2
+    rows, columns = partial.shape
+    held = partial.reshape((2,) * len(bits) + (rows // total, columns))
+    for place, bit in enumerate(bits):
+        dim = len(bits) - 1 - place
+        low = lax.index_in_dim(held, 0, dim, keepdims=False)
+        high = lax.index_in_dim(held, 1, dim, keepdims=False)
+        upper = (mine // bit) % 2 == 1
+        keep = jnp.where(upper, high, low)
+        send = jnp.where(upper, low, high).astype(jnp.bfloat16)
+        got = lax.ppermute(send, axes, [(i, i ^ bit) for i in range(total)])
+        held = keep + got.astype(jnp.float32)
+    return held
 
 
 def padded(x, sides, width):
@@ -34,17 +67,6 @@
         after = lax.ppermute(leading, axis, down)
         x = jnp.concatenate([before, x, after], axis=dim)
     return x
-
-
-def carry_combine(earlier, following):
-    gain_out = (earlier[0].astype(jnp.float32) * following[0].astype(jnp.float32)).astype(
-        jnp.bfloat16
-    )
-    state_out = (
-        following[0].astype(jnp.float32)[:, None, None] * earlier[1].astype(jnp.float32)
-        + following[1].astype(jnp.float32)
-    ).astype(jnp.bfloat16)
-    return (gain_out, state_out)
 
 
 def block_terms(values, keys_in, reads, logdec, user_row, before_user, after_user):
@@ -103,14 +125,8 @@
     inner, cumulative, fwd_gain, fwd_state, rev_gain, rev_state = block_terms(
         values, keys_in, reads, logdec, user_row, before_user, after_user
     )
-    neutral = jnp.ones_like(fwd_gain)
-    nothing = jnp.zeros_like(fwd_state)
-    from_before = carried_in(
-        (fwd_gain, fwd_state), "ctx", carry_combine, (neutral, nothing), False
-    )[1]
-    from_after = carried_in((rev_gain, rev_state), "ctx", carry_combine, (neutral, nothing), True)[
-        1
-    ]
+    from_before = carried_in(fwd_gain, fwd_state, "ctx", False)
+    from_after = carried_in(rev_gain, rev_state, "ctx", True)
     return apply_carries(
         inner, reads, cumulative, user_row, before_user, after_user, from_before, from_after
     )
@@ -154,13 +170,11 @@
     )
     grad_mixed = pullback(grad_normed)[0].astype(jnp.bfloat16)
     grad_feat = mix_local(grad_mixed, reads, keys_in, logdec, user_row, before_user, after_user)
-    weight_grad = lax.psum_scatter(
+    weight_grad = summed_rows(
         lax.dot_general(
             normed_out, grad_local, (((0,), (0,)), ((), ())), preferred_element_type=jnp.float32
         ),
         ("dp", "ctx"),
-        scatter_dimension=0,
-        tiled=True,
     )
     return (result.astype(jnp.bfloat16)[None], grad_feat.astype(jnp.bfloat16)[None], weight_grad)
 

time: 403 us -> 134 us (0.33)
  waiting for transfers between devices: 212 us -> 17.9 us
  other arithmetic: 104 us -> 17.9 us
  starting transfers between devices: 4.41 us -> 62.2 us
  blocking collectives: 36.1 us -> 0 us
  matrix products: 13.7 us -> 9.53 us
    reduce_scatter x1 -> x0, waiting for transfers between devices: 112 us -> none  [local(): lax.psum_scatter(lax.dot_general(normed_out, grad_local, (((0,), (0,)), (...]
    all_gather x4 -> x0, waiting for transfers between devices: 71.2 us -> none  [carried_in(): pieces = jax.tree.map(lambda part: lax.all_gather(part, axis), value)]
    ppermute x0 -> x21, starting transfers between devices: none -> 57.9 us  [the longest x16 46.3 us: shifted(): return lax.ppermute(value, axis, pairs)]
    select_n x60 -> x0, other arithmetic: 44.8 us -> none  [step(): jnp.where(position < mine, new, old)]
    convert_element_type x62 -> x32, other arithmetic: 48 us -> 6.67 us  [the longest x12 2.28 us: carried_in(): state = (wide[:, None, None] * far[:, :-8].astype(jnp.float32) + state.as...]
    unnamed x1 -> x0, blocking collectives: 36.1 us -> none
    all_gather x1, waiting for transfers between devices: 28.3 us -> 1.17 us  [local(): full_weight = lax.all_gather(out_weight, ('dp', 'ctx'), axis=0, tiled=True)]
    ppermute x0 -> x21, waiting for transfers between devices: none -> 16.1 us  [the longest x16 8.31 us: shifted(): return lax.ppermute(value, axis, pairs)]
  transfers between devices with their start and end apart: 8 -> 24, of which waited for: 5 -> 9; matrix products, arithmetic and copies ran while one was open for 29% -> 23% of each run, Pallas kernels for 0% -> 0%
where the time goes in v1:
time: 134 us; the launch traced here: 132 us
  starting transfers between devices  62.2 us (46%)
  waiting for transfers between devices  17.9 us (13%)
  other arithmetic  17.9 us (13%)
  between operations  17.4 us (13%)
  matrix products  9.53 us (7%)
  local copies, waits for them, and re-layouts  7.3 us (5%)
    ppermute x16, starting transfers between devices, shifted(): return lax.ppermute(value, axis, pairs)  46.3 us
    ppermute x5, starting transfers between devices, summed_rows(): got = lax.ppermute(send, axes, [(i, i ^ bit) for i in range(total)])  11.6 us
    ppermute x16, waiting for transfers between devices, shifted(): return lax.ppermute(value, axis, pairs)  8.31 us
    ppermute x5, waiting for transfers between devices, summed_rows(): got = lax.ppermute(send, axes, [(i, i ^ bit) for i in range(total)])  7.78 us
    ppermute x1, starting transfers between devices, padded(): before = lax.ppermute(last, axis, up)  2.93 us
  transfers between devices with their start and end apart: 24, of which 9 were waited for; matrix products, arithmetic and copies ran while one was open for 23% of the time, Pallas kernels for 0%

profile of v1, /device:TPU:0, one launch (start us, length us, event | category | flops | bytes accessed | tf_op | source)
XLA Modules:
  0.0 132.2 jit_solution(1151225759714910840)
XLA Ops:
  7.2 0.7 all-gather.2.cloned.1.call-update
  7.9 0.7 broadcast_add_fusion
  8.6 0.6 fusion.107
  9.2 2.9 %collective-permute-start = (s32[1,1]{1,0:T(1,128)}, s32[1,1]{1,0:T(1,128)}, u32[]{:S(2)}, u32[]{:S(2)}) collective-permute-start(s32[1,1]{1,0:T(1,128)} %get-tuple-element.44), channel_id=1, source_target_pairs={{0,1},{1,2},{2,3},{3,4},{4,5},{5,6},{6,7},{7,8},{8,9},{9,10},{10,1... | collective-permute-start | bytes 20 | tf_op jit(solution)/shard_map/ppermute | solution.py:66
  12.1 1.3 collective-permute-start.1
  13.5 1.3 fusion.106
  14.8 0.7 bitcast_convert_fusion
  15.5 0.7 bitcast_convert_fusion.1
  16.2 1.5 %convolution_multiply_fusion.1 = f32[128,128]{1,0:T(8,128)} fusion(bf16[1,128,64]{1,2,0:T(8,128)(2,1)} %param.12, bf16[1,128,64]{1,2,0:T(8,128)(2,1)} %param.13), kind=kOutput, calls=%fused_computation.22 | convolution fusion | flops 2162688 | bytes 98304 | tf_op jit(solution)/shard_map/dot_general | solution.py:77
  17.8 0.9 convolution_multiply_fusion.2
  18.8 0.7 convert_element_type.545
  19.5 0.8 broadcast_compare_fusion
  20.3 1.0 copy.79
  21.3 1.1 copy.49
  22.4 0.8 bitcast_multiply_fusion.1
  23.1 0.3 reduce_window_sum.12
  23.4 0.5 convolution_bitcast_fusion.5
  23.9 1.4 %add_add_fusion.1 = s32[1,130]{1,0:T(1,128)S(1)} fusion(s32[1,1]{1,0:T(1,128)} %collective-permute-done.1, s32[1,128]{1,0:T(1,128)S(1)} %broadcast_add_fusion, s32[1,1]{1,0:T(1,128)} %collective-permute-done), kind=kLoop, calls=%fused_computation.181 | loop fusion | flops 390 | bytes 1040 | tf_op jit(solution)/shard_map/sub | solution.py:147
  25.3 0.6 fusion.105
  28.4 2.5 %fusion.90 = (f32[128]{0:T(128)S(1)}, f32[128]{0:T(128)S(1)}, f32[128]{0:T(128)S(1)}, f32[128]{0:T(128)S(1)}) fusion(s32[1,128]{1,0:T(1,128)S(1)} %copy-done.11, s32[]{:T(128)} %bitcast.5, s32[]{:T(128)} %bitcast.14, s32[]{:T(128)} %bitcast.8, s32[]{:T(128)} %bitcast.17), kind=kLoop, calls=%fused_computation.182 | loop fusion | flops 1024 | bytes 2576 | tf_op jit(solution)/shard_map/mul | solution.py:111
  31.5 1.3 collective-permute-start.6
  33.1 5.3 %collective-permute-start.2 = (bf16[8,72,128]{2,1,0:T(8,128)(2,1)S(1)}, bf16[8,72,128]{2,1,0:T(8,128)(2,1)S(1)}, u32[]{:S(2)}, u32[]{:S(2)}) collective-permute-start(bf16[8,72,128]{2,1,0:T(8,128)(2,1)S(1)} %pad_maximum_fusion.1), channel_id=1, source_target_pairs={{0,1},{1,2},{2,3},{3,4},{4,5},{5,6},{6,7},{7,8},{8,9},{9,10},{10,1... | collective-permute-start | bytes 442376 | tf_op jit(solution)/shard_map/ppermute | solution.py:18
  38.9 1.3 collective-permute-start.7
  40.7 6.8 %collective-permute-start.3 = (bf16[8,72,128]{2,1,0:T(8,128)(2,1)S(1)}, bf16[8,72,128]{2,1,0:T(8,128)(2,1)S(1)}, u32[]{:S(2)}, u32[]{:S(2)}) collective-permute-start(bf16[8,72,128]{2,1,0:T(8,128)(2,1)S(1)} %pad_maximum_fusion.4), channel_id=1, source_target_pairs={{0,2},{1,3},{2,4},{3,5},{4,6},{5,7},{6,8},{7,9},{8,10},{9,11},{10,... | collective-permute-start | bytes 442376 | tf_op jit(solution)/shard_map/ppermute | solution.py:18
  47.9 1.3 collective-permute-start.8
  49.2 3.0 %collective-permute-done.3 = bf16[8,72,128]{2,1,0:T(8,128)(2,1)S(1)} collective-permute-done((bf16[8,72,128]{2,1,0:T(8,128)(2,1)S(1)}, bf16[8,72,128]{2,1,0:T(8,128)(2,1)S(1)}, u32[]{:S(2)}, u32[]{:S(2)}) %collective-permute-start.3) | collective-permute-done | bytes 147488 | tf_op jit(solution)/shard_map/ppermute | solution.py:18
  52.6 6.2 %collective-permute-start.4 = (bf16[8,72,128]{2,1,0:T(8,128)(2,1)S(1)}, bf16[8,72,128]{2,1,0:T(8,128)(2,1)S(1)}, u32[]{:S(2)}, u32[]{:S(2)}) collective-permute-start(bf16[8,72,128]{2,1,0:T(8,128)(2,1)S(1)} %pad_maximum_fusion.5), channel_id=1, source_target_pairs={{0,4},{1,5},{2,6},{3,7},{4,8},{5,9},{6,10},{7,11},{8,12},{9,13},{1... | collective-permute-start | bytes 442376 | tf_op jit(solution)/shard_map/ppermute | solution.py:18
  58.9 1.3 collective-permute-start.9
  60.2 3.0 %collective-permute-done.4 = bf16[8,72,128]{2,1,0:T(8,128)(2,1)S(1)} collective-permute-done((bf16[8,72,128]{2,1,0:T(8,128)(2,1)S(1)}, bf16[8,72,128]{2,1,0:T(8,128)(2,1)S(1)}, u32[]{:S(2)}, u32[]{:S(2)}) %collective-permute-start.4) | collective-permute-done | bytes 147488 | tf_op jit(solution)/shard_map/ppermute | solution.py:18
  63.4 1.3 collective-permute-start.5
  65.0 0.7 collective-permute-done.5
  65.6 0.4 multiply_reduce_fusion.1
  66.2 1.2 all-gather.2.cloned.1.call-done
  67.4 1.8 %multiply_reduce_fusion = (f32[128]{0:T(128)S(1)}, f32[128,1024]{1,0:T(8,128)S(1)}) fusion(f32[128,1024]{1,0:T(8,128)S(1)} %copy.48, bf16[1,128,1024]{2,1,0:T(8,128)(2,1)S(1)} %copy-done.1, f32[1024]{0:T(1024)S(1)} %convert_element_type.545, bf16[1024,512]{1,0:T(8,128)(2,1)} %all-gather.2.cloned.1.call-done, bf16[1,128,512]{2,1,0:T(8,128)(2,1)S(1)} %copy-done), kind=kOutput, calls=%fused_computation.42 | convolution fusion | flops 135397248 | bytes 2494976 | tf_op jit(solution)/shard_map/dot_general | solution.py:168
  69.2 0.3 fusion.97
  69.9 0.8 copy.55
  70.8 0.7 pad_maximum_fusion
  71.5 1.4 %collective-permute-start.14 = (bf16[8,72,128]{2,1,0:T(8,128)(2,1)S(1)}, bf16[8,72,128]{2,1,0:T(8,128)(2,1)S(1)}, u32[]{:S(2)}, u32[]{:S(2)}) collective-permute-start(bf16[8,72,128]{2,1,0:T(8,128)(2,1)S(1)} %pad_maximum_fusion.2), channel_id=1, source_target_pairs={{1,0},{2,1},{3,2},{4,3},{5,4},{6,5},{7,6},{8,7},{9,8},{10,9},{11,1... | collective-permute-start | bytes 442376 | tf_op jit(solution)/shard_map/ppermute | solution.py:18
  72.9 3.7 %collective-permute-start.10 = (bf16[8,72,128]{2,1,0:T(8,128)(2,1)}, bf16[8,72,128]{2,1,0:T(8,128)(2,1)}, u32[]{:S(2)}, u32[]{:S(2)}) collective-permute-start(bf16[8,72,128]{2,1,0:T(8,128)(2,1)} %pad_maximum_fusion), channel_id=1, source_target_pairs={{0,1},{1,2},{2,3},{3,4},{4,5},{5,6},{6,7},{7,8},{8,9},{9,10},{10,1... | collective-permute-start | bytes 442376 | tf_op jit(solution)/shard_map/ppermute | solution.py:18
  76.6 1.4 %fusion.46 = f32[2,2,2,2,2,32,512]{6,5,4,3,2,1,0:T(8,128)S(1)} fusion(bf16[2,2,2,2,2,32,128]{6,5,4,3,2,1,0:T(8,128)(2,1)} %bitcast.230, bf16[1,128,512]{2,1,0:T(8,128)(2,1)S(1)} %copy-done), kind=kOutput, calls=%fused_computation.104 | convolution fusion | flops 134217728 | bytes 2490368 | tf_op jit(solution)/shard_map/dot_general | solution.py:174
  78.0 0.9 fusion.14
  78.9 1.8 %collective-permute-start.18 = (bf16[2,2,2,2,32,512]{5,4,3,2,1,0:T(8,128)(2,1)}, bf16[2,2,2,2,32,512]{5,4,3,2,1,0:T(8,128)(2,1)}, u32[]{:S(2)}, u32[]{:S(2)}) collective-permute-start(bf16[2,2,2,2,32,512]{5,4,3,2,1,0:T(8,128)(2,1)} %fusion.14), channel_id=1, source_target_pairs={{0,1},{1,0},{2,3},{3,2},{4,5},{5,4},{6,7},{7,6},{8,9},{9,8},{10,11... | collective-permute-start | bytes 1572872 | tf_op jit(solution)/shard_map/ppermute | solution.py:54
  80.7 1.0 fusion.9
  81.7 0.5 convolution_bitcast_fusion.2
  82.7 1.3 collective-permute-start.15
  84.0 1.0 add_convert_fusion.5
  85.1 0.9 convert_reduce_fusion.1
  86.2 7.4 %collective-permute-start.11 = (bf16[8,72,128]{2,1,0:T(8,128)(2,1)S(1)}, bf16[8,72,128]{2,1,0:T(8,128)(2,1)S(1)}, u32[]{:S(2)}, u32[]{:S(2)}) collective-permute-start(bf16[8,72,128]{2,1,0:T(8,128)(2,1)S(1)} %pad_maximum_fusion.8), channel_id=1, source_target_pairs={{0,2},{1,3},{2,4},{3,5},{4,6},{5,7},{6,8},{7,9},{8,10},{9,11},{10,... | collective-permute-start | bytes 442376 | tf_op jit(solution)/shard_map/ppermute | solution.py:18
  94.0 1.3 collective-permute-start.16
  95.3 1.6 %collective-permute-done.11 = bf16[8,72,128]{2,1,0:T(8,128)(2,1)S(1)} collective-permute-done((bf16[8,72,128]{2,1,0:T(8,128)(2,1)S(1)}, bf16[8,72,128]{2,1,0:T(8,128)(2,1)S(1)}, u32[]{:S(2)}, u32[]{:S(2)}) %collective-permute-start.11) | collective-permute-done | bytes 147488 | tf_op jit(solution)/shard_map/ppermute | solution.py:18
  97.2 1.3 fusion.11
  98.5 2.7 %collective-permute-start.19 = (bf16[2,2,2,32,512]{4,3,2,1,0:T(8,128)(2,1)S(1)}, bf16[2,2,2,32,512]{4,3,2,1,0:T(8,128)(2,1)S(1)}, u32[]{:S(2)}, u32[]{:S(2)}) collective-permute-start(bf16[2,2,2,32,512]{4,3,2,1,0:T(8,128)(2,1)S(1)} %fusion.20), channel_id=1, source_target_pairs={{0,2},{1,3},{2,0},{3,1},{4,6},{5,7},{6,4},{7,5},{8,10},{9,11},{10,... | collective-permute-start | bytes 786440 | tf_op jit(solution)/shard_map/ppermute | solution.py:54
  101.4 3.8 %collective-permute-start.12 = (bf16[8,72,128]{2,1,0:T(8,128)(2,1)S(1)}, bf16[8,72,128]{2,1,0:T(8,128)(2,1)S(1)}, u32[]{:S(2)}, u32[]{:S(2)}) collective-permute-start(bf16[8,72,128]{2,1,0:T(8,128)(2,1)S(1)} %pad_maximum_fusion.9), channel_id=1, source_target_pairs={{0,4},{1,5},{2,6},{3,7},{4,8},{5,9},{6,10},{7,11},{8,12},{9,13},{1... | collective-permute-start | bytes 442376 | tf_op jit(solution)/shard_map/ppermute | solution.py:18
  105.4 1.3 collective-permute-start.17
  106.9 3.6 %collective-permute-start.20 = (bf16[2,2,32,512]{3,2,1,0:T(8,128)(2,1)S(1)}, bf16[2,2,32,512]{3,2,1,0:T(8,128)(2,1)S(1)}, u32[]{:S(2)}, u32[]{:S(2)}) collective-permute-start(bf16[2,2,32,512]{3,2,1,0:T(8,128)(2,1)S(1)} %fusion.43), channel_id=1, source_target_pairs={{0,4},{1,5},{2,6},{3,7},{4,0},{5,1},{6,2},{7,3},{8,12},{9,13},{10,... | collective-permute-start | bytes 393224 | tf_op jit(solution)/shard_map/ppermute | solution.py:54
  110.6 1.3 collective-permute-start.13
  111.9 2.7 %collective-permute-done.20 = bf16[2,2,32,512]{3,2,1,0:T(8,128)(2,1)S(1)} collective-permute-done((bf16[2,2,32,512]{3,2,1,0:T(8,128)(2,1)S(1)}, bf16[2,2,32,512]{3,2,1,0:T(8,128)(2,1)S(1)}, u32[]{:S(2)}, u32[]{:S(2)}) %collective-permute-start.20) | collective-permute-done | bytes 131104 | tf_op jit(solution)/shard_map/ppermute | solution.py:54
  114.8 2.1 %collective-permute-start.21 = (bf16[2,32,512]{2,1,0:T(8,128)(2,1)S(1)}, bf16[2,32,512]{2,1,0:T(8,128)(2,1)S(1)}, u32[]{:S(2)}, u32[]{:S(2)}) collective-permute-start(bf16[2,32,512]{2,1,0:T(8,128)(2,1)S(1)} %fusion.58), channel_id=1, source_target_pairs={{0,8},{1,9},{2,10},{3,11},{4,12},{5,13},{6,14},{7,15},{8,0},{9,1},... | collective-permute-start | bytes 196616 | tf_op jit(solution)/shard_map/ppermute | solution.py:54
  117.1 3.5 %collective-permute-done.21 = bf16[2,32,512]{2,1,0:T(8,128)(2,1)S(1)} collective-permute-done((bf16[2,32,512]{2,1,0:T(8,128)(2,1)S(1)}, bf16[2,32,512]{2,1,0:T(8,128)(2,1)S(1)}, u32[]{:S(2)}, u32[]{:S(2)}) %collective-permute-start.21) | collective-permute-done | bytes 65568 | tf_op jit(solution)/shard_map/ppermute | solution.py:54
  120.7 1.4 %collective-permute-start.22 = (bf16[32,512]{1,0:T(8,128)(2,1)S(1)}, bf16[32,512]{1,0:T(8,128)(2,1)S(1)}, u32[]{:S(2)}, u32[]{:S(2)}) collective-permute-start(bf16[32,512]{1,0:T(8,128)(2,1)S(1)} %fusion.59), channel_id=1, source_target_pairs={{0,16},{1,17},{2,18},{3,19},{4,20},{5,21},{6,22},{7,23},{8,24},{9,... | collective-permute-start | bytes 98312 | tf_op jit(solution)/shard_map/ppermute | solution.py:54
  122.2 0.3 fusion.8
  122.4 0.9 copy.72
  123.3 1.4 %collective-permute-done.22 = bf16[32,512]{1,0:T(8,128)(2,1)S(1)} collective-permute-done((bf16[32,512]{1,0:T(8,128)(2,1)S(1)}, bf16[32,512]{1,0:T(8,128)(2,1)S(1)}, u32[]{:S(2)}, u32[]{:S(2)}) %collective-permute-start.22) | collective-permute-done | bytes 32800 | tf_op jit(solution)/shard_map/ppermute | solution.py:54
  124.7 0.6 bitcast_add_fusion
  (118 shorter events, 6.2 us)
Async XLA Ops:
  7.2 60.2 %copy-start = (bf16[1,128,512]{2,1,0:T(8,128)(2,1)S(1)}, bf16[1,128,512]{2,1,0:T(8,128)(2,1)}, u32[]{:S(2)}) copy-start(bf16[1,128,512]{2,1,0:T(8,128)(2,1)} %param.19) | copy-start | bytes 393220
  7.2 21.2 %copy-start.11 = (s32[1,128]{1,0:T(1,128)S(1)}, s32[1,128]{1,0:T(1,128)}, u32[]{:S(2)}) copy-start(s32[1,128]{1,0:T(1,128)} %param.16) | copy-start | bytes 1540
  7.2 60.2 %all-gather.2.cloned.1.call-start = ((), (), s32[]{:S(2)}) async-start(), calls=%async_computation | async-start | bytes 1081344 | tf_op jit(solution)/shard_map/all_gather | solution.py:166
  9.2 14.7 %collective-permute-start = (s32[1,1]{1,0:T(1,128)}, s32[1,1]{1,0:T(1,128)}, u32[]{:S(2)}, u32[]{:S(2)}) collective-permute-start(s32[1,1]{1,0:T(1,128)} %get-tuple-element.44), channel_id=1, source_target_pairs={{0,1},{1,2},{2,3},{3,4},{4,5},{5,6},{6,7},{7,8},{8,9},{9,10},{10,1... | collective-permute-start | bytes 20 | tf_op jit(solution)/shard_map/ppermute | solution.py:66
  12.1 11.8 %collective-permute-start.1 = (s32[1,1]{1,0:T(1,128)}, s32[1,1]{1,0:T(1,128)}, u32[]{:S(2)}, u32[]{:S(2)}) collective-permute-start(s32[1,1]{1,0:T(1,128)} %get-tuple-element.45), channel_id=1, source_target_pairs={{1,0},{2,1},{3,2},{4,3},{5,4},{6,5},{7,6},{8,7},{9,8},{10,9},{11,1... | collective-permute-start | bytes 20 | tf_op jit(solution)/shard_map/ppermute | solution.py:67
  19.5 49.7 %copy-start.5 = (f32[1024]{0:T(1024)}, f32[1024]{0:T(1024)S(1)}, u32[]{:S(2)}) copy-start(f32[1024]{0:T(1024)S(1)} %convert_element_type.545) | copy-start | bytes 12292
  20.3 12.5 %copy-start.9 = (pred[128,128]{1,0:T(8,128)(4,1)}, pred[128,128]{1,0:T(8,128)(4,1)S(1)}, u32[]{:S(2)}) copy-start(pred[128,128]{1,0:T(8,128)(4,1)S(1)} %broadcast_compare_fusion) | copy-start | bytes 49156
  31.0 7.4 %copy-start.13 = (f32[8]{0:T(128)}, f32[8]{0:T(128)S(1)}, u32[]{:S(2)}) copy-start(f32[8]{0:T(128)S(1)} %get-tuple-element.40) | copy-start | bytes 100
  31.1 21.5 %copy-start.12 = (f32[8]{0:T(128)}, f32[8]{0:T(128)S(1)}, u32[]{:S(2)}) copy-start(f32[8]{0:T(128)S(1)} %get-tuple-element.15) | copy-start | bytes 100
  31.1 34.5 %copy-start.7 = (f32[128,8]{0,1:T(8,128)}, f32[128,8]{0,1:T(8,128)S(1)}, u32[]{:S(2)}) copy-start(f32[128,8]{0,1:T(8,128)S(1)} %get-tuple-element.25) | copy-start | bytes 12292
  31.5 6.9 %collective-permute-start.6 = (bf16[8,72,128]{2,1,0:T(8,128)(2,1)S(1)}, bf16[8,72,128]{2,1,0:T(8,128)(2,1)S(1)}, u32[]{:S(2)}, u32[]{:S(2)}) collective-permute-start(bf16[8,72,128]{2,1,0:T(8,128)(2,1)S(1)} %pad_maximum_fusion.3), channel_id=1, source_target_pairs={{1,0},{2,1},{3,2},{4,3},{5,4},{6,5},{7,6},{8,7},{9,8},{10,9},{11,1... | collective-permute-start | bytes 442376 | tf_op jit(solution)/shard_map/ppermute | solution.py:18
  33.0 31.7 %copy-start.3 = (bf16[1,128,64]{1,2,0:T(8,128)(2,1)S(1)}, bf16[1,128,64]{1,2,0:T(8,128)(2,1)}, u32[]{:S(2)}) copy-start(bf16[1,128,64]{1,2,0:T(8,128)(2,1)} %param.13) | copy-start | bytes 49156
  33.1 7.1 %collective-permute-start.2 = (bf16[8,72,128]{2,1,0:T(8,128)(2,1)S(1)}, bf16[8,72,128]{2,1,0:T(8,128)(2,1)S(1)}, u32[]{:S(2)}, u32[]{:S(2)}) collective-permute-start(bf16[8,72,128]{2,1,0:T(8,128)(2,1)S(1)} %pad_maximum_fusion.1), channel_id=1, source_target_pairs={{0,1},{1,2},{2,3},{3,4},{4,5},{5,6},{6,7},{7,8},{8,9},{9,10},{10,1... | collective-permute-start | bytes 442376 | tf_op jit(solution)/shard_map/ppermute | solution.py:18
  38.9 8.6 %collective-permute-start.7 = (bf16[8,72,128]{2,1,0:T(8,128)(2,1)S(1)}, bf16[8,72,128]{2,1,0:T(8,128)(2,1)S(1)}, u32[]{:S(2)}, u32[]{:S(2)}) collective-permute-start(bf16[8,72,128]{2,1,0:T(8,128)(2,1)S(1)} %pad_maximum_fusion.6), channel_id=1, source_target_pairs={{2,0},{3,1},{4,2},{5,3},{6,4},{7,5},{8,6},{9,7},{10,8},{11,9},{12,... | collective-permute-start | bytes 442376 | tf_op jit(solution)/shard_map/ppermute | solution.py:18
  40.7 11.5 %collective-permute-start.3 = (bf16[8,72,128]{2,1,0:T(8,128)(2,1)S(1)}, bf16[8,72,128]{2,1,0:T(8,128)(2,1)S(1)}, u32[]{:S(2)}, u32[]{:S(2)}) collective-permute-start(bf16[8,72,128]{2,1,0:T(8,128)(2,1)S(1)} %pad_maximum_fusion.4), channel_id=1, source_target_pairs={{0,2},{1,3},{2,4},{3,5},{4,6},{5,7},{6,8},{7,9},{8,10},{9,11},{10,... | collective-permute-start | bytes 442376 | tf_op jit(solution)/shard_map/ppermute | solution.py:18
  47.9 10.9 %collective-permute-start.8 = (bf16[8,72,128]{2,1,0:T(8,128)(2,1)S(1)}, bf16[8,72,128]{2,1,0:T(8,128)(2,1)S(1)}, u32[]{:S(2)}, u32[]{:S(2)}) collective-permute-start(bf16[8,72,128]{2,1,0:T(8,128)(2,1)S(1)} %pad_maximum_fusion.7), channel_id=1, source_target_pairs={{4,0},{5,1},{6,2},{7,3},{8,4},{9,5},{10,6},{11,7},{12,8},{13,9},{1... | collective-permute-start | bytes 442376 | tf_op jit(solution)/shard_map/ppermute | solution.py:18
  52.6 10.7 %collective-permute-start.4 = (bf16[8,72,128]{2,1,0:T(8,128)(2,1)S(1)}, bf16[8,72,128]{2,1,0:T(8,128)(2,1)S(1)}, u32[]{:S(2)}, u32[]{:S(2)}) collective-permute-start(bf16[8,72,128]{2,1,0:T(8,128)(2,1)S(1)} %pad_maximum_fusion.5), channel_id=1, source_target_pairs={{0,4},{1,5},{2,6},{3,7},{4,8},{5,9},{6,10},{7,11},{8,12},{9,13},{1... | collective-permute-start | bytes 442376 | tf_op jit(solution)/shard_map/ppermute | solution.py:18
  58.9 5.7 %collective-permute-start.9 = (bf16[8,64,128]{2,1,0:T(8,128)(2,1)S(1)}, bf16[8,64,128]{2,1,0:T(8,128)(2,1)S(1)}, u32[]{:S(2)}, u32[]{:S(2)}) collective-permute-start(bf16[8,64,128]{2,1,0:T(8,128)(2,1)S(1)} %add_convert_fusion.6), channel_id=1, source_target_pairs={{1,0},{2,1},{3,2},{4,3},{5,4},{6,5},{7,6},{8,7},{9,8},{10,9},{11,1... | collective-permute-start | bytes 393224 | tf_op jit(solution)/shard_map/ppermute | solution.py:18
  63.4 2.3 %collective-permute-start.5 = (bf16[8,64,128]{2,1,0:T(8,128)(2,1)S(1)}, bf16[8,64,128]{2,1,0:T(8,128)(2,1)S(1)}, u32[]{:S(2)}, u32[]{:S(2)}) collective-permute-start(bf16[8,64,128]{2,1,0:T(8,128)(2,1)S(1)} %add_convert_fusion.9), channel_id=1, source_target_pairs={{0,1},{1,2},{2,3},{3,4},{4,5},{5,6},{6,7},{7,8},{8,9},{9,10},{10,1... | collective-permute-start | bytes 393224 | tf_op jit(solution)/shard_map/ppermute | solution.py:18
  65.0 2.4 %copy-start.1 = (bf16[1,128,1024]{2,1,0:T(8,128)(2,1)S(1)}, bf16[1,128,1024]{2,1,0:T(8,128)(2,1)}, u32[]{:S(2)}) copy-start(bf16[1,128,1024]{2,1,0:T(8,128)(2,1)} %param.11) | copy-start | bytes 786436
  69.2 7.4 %copy-start.15 = (f32[128]{0:T(128)}, f32[128]{0:T(128)S(1)}, u32[]{:S(2)}) copy-start(f32[128]{0:T(128)S(1)} %get-tuple-element.35) | copy-start | bytes 1540
  71.4 9.2 %copy-start.6 = (f32[1024]{0:T(1024)S(1)}, f32[1024]{0:T(1024)}, u32[]{:S(2)}) copy-start(f32[1024]{0:T(1024)} %copy-done.5) | copy-start | bytes 12292
  71.5 9.2 %copy-start.17 = (bf16[1024,512]{1,0:T(8,128)(2,1)S(1)}, bf16[1024,512]{1,0:T(8,128)(2,1)}, u32[]{:S(2)}) copy-start(bf16[1024,512]{1,0:T(8,128)(2,1)} %all-gather.2.cloned.1.call-done) | copy-start | bytes 3145732
  71.5 10.7 %collective-permute-start.14 = (bf16[8,72,128]{2,1,0:T(8,128)(2,1)S(1)}, bf16[8,72,128]{2,1,0:T(8,128)(2,1)S(1)}, u32[]{:S(2)}, u32[]{:S(2)}) collective-permute-start(bf16[8,72,128]{2,1,0:T(8,128)(2,1)S(1)} %pad_maximum_fusion.2), channel_id=1, source_target_pairs={{1,0},{2,1},{3,2},{4,3},{5,4},{6,5},{7,6},{8,7},{9,8},{10,9},{11,1... | collective-permute-start | bytes 442376 | tf_op jit(solution)/shard_map/ppermute | solution.py:18
  72.9 11.1 %collective-permute-start.10 = (bf16[8,72,128]{2,1,0:T(8,128)(2,1)}, bf16[8,72,128]{2,1,0:T(8,128)(2,1)}, u32[]{:S(2)}, u32[]{:S(2)}) collective-permute-start(bf16[8,72,128]{2,1,0:T(8,128)(2,1)} %pad_maximum_fusion), channel_id=1, source_target_pairs={{0,1},{1,2},{2,3},{3,4},{4,5},{5,6},{6,7},{7,8},{8,9},{9,10},{10,1... | collective-permute-start | bytes 442376 | tf_op jit(solution)/shard_map/ppermute | solution.py:18
  76.6 4.1 %copy-start.16 = (f32[128]{0:T(128)S(1)}, f32[128]{0:T(128)}, u32[]{:S(2)}) copy-start(f32[128]{0:T(128)} %copy-done.15) | copy-start | bytes 1540
  78.9 2.8 %copy-start.4 = (f32[128,128]{1,0:T(8,128)S(1)}, f32[128,128]{1,0:T(8,128)}, u32[]{:S(2)}) copy-start(f32[128,128]{1,0:T(8,128)} %convolution_multiply_fusion.1) | copy-start | bytes 196612
  78.9 2.8 %copy-start.10 = (pred[128,128]{1,0:T(8,128)(4,1)S(1)}, pred[128,128]{1,0:T(8,128)(4,1)}, u32[]{:S(2)}) copy-start(pred[128,128]{1,0:T(8,128)(4,1)} %copy-done.9) | copy-start | bytes 49156
  78.9 3.3 %copy-start.14 = (f32[8]{0:T(128)S(1)}, f32[8]{0:T(128)}, u32[]{:S(2)}) copy-start(f32[8]{0:T(128)} %copy-done.13) | copy-start | bytes 100
  78.9 18.3 %collective-permute-start.18 = (bf16[2,2,2,2,32,512]{5,4,3,2,1,0:T(8,128)(2,1)}, bf16[2,2,2,2,32,512]{5,4,3,2,1,0:T(8,128)(2,1)}, u32[]{:S(2)}, u32[]{:S(2)}) collective-permute-start(bf16[2,2,2,2,32,512]{5,4,3,2,1,0:T(8,128)(2,1)} %fusion.14), channel_id=1, source_target_pairs={{0,1},{1,0},{2,3},{3,2},{4,5},{5,4},{6,7},{7,6},{8,9},{9,8},{10,11... | collective-permute-start | bytes 1572872 | tf_op jit(solution)/shard_map/ppermute | solution.py:54
  82.7 10.9 %collective-permute-start.15 = (bf16[8,72,128]{2,1,0:T(8,128)(2,1)S(1)}, bf16[8,72,128]{2,1,0:T(8,128)(2,1)S(1)}, u32[]{:S(2)}, u32[]{:S(2)}) collective-permute-start(bf16[8,72,128]{2,1,0:T(8,128)(2,1)S(1)} %pad_maximum_fusion.10), channel_id=1, source_target_pairs={{2,0},{3,1},{4,2},{5,3},{6,4},{7,5},{8,6},{9,7},{10,8},{11,9},{12,... | collective-permute-start | bytes 442376 | tf_op jit(solution)/shard_map/ppermute | solution.py:18
  86.2 10.7 %collective-permute-start.11 = (bf16[8,72,128]{2,1,0:T(8,128)(2,1)S(1)}, bf16[8,72,128]{2,1,0:T(8,128)(2,1)S(1)}, u32[]{:S(2)}, u32[]{:S(2)}) collective-permute-start(bf16[8,72,128]{2,1,0:T(8,128)(2,1)S(1)} %pad_maximum_fusion.8), channel_id=1, source_target_pairs={{0,2},{1,3},{2,4},{3,5},{4,6},{5,7},{6,8},{7,9},{8,10},{9,11},{10,... | collective-permute-start | bytes 442376 | tf_op jit(solution)/shard_map/ppermute | solution.py:18
  94.0 11.2 %collective-permute-start.16 = (bf16[8,72,128]{2,1,0:T(8,128)(2,1)S(1)}, bf16[8,72,128]{2,1,0:T(8,128)(2,1)S(1)}, u32[]{:S(2)}, u32[]{:S(2)}) collective-permute-start(bf16[8,72,128]{2,1,0:T(8,128)(2,1)S(1)} %pad_maximum_fusion.11), channel_id=1, source_target_pairs={{4,0},{5,1},{6,2},{7,3},{8,4},{9,5},{10,6},{11,7},{12,8},{13,9},{1... | collective-permute-start | bytes 442376 | tf_op jit(solution)/shard_map/ppermute | solution.py:18
  98.5 8.2 %collective-permute-start.19 = (bf16[2,2,2,32,512]{4,3,2,1,0:T(8,128)(2,1)S(1)}, bf16[2,2,2,32,512]{4,3,2,1,0:T(8,128)(2,1)S(1)}, u32[]{:S(2)}, u32[]{:S(2)}) collective-permute-start(bf16[2,2,2,32,512]{4,3,2,1,0:T(8,128)(2,1)S(1)} %fusion.20), channel_id=1, source_target_pairs={{0,2},{1,3},{2,0},{3,1},{4,6},{5,7},{6,4},{7,5},{8,10},{9,11},{10,... | collective-permute-start | bytes 786440 | tf_op jit(solution)/shard_map/ppermute | solution.py:54
  101.3 15.5 %copy-start.2 = (bf16[1,128,64]{1,2,0:T(8,128)(2,1)S(1)}, bf16[1,128,64]{1,2,0:T(8,128)(2,1)}, u32[]{:S(2)}) copy-start(bf16[1,128,64]{1,2,0:T(8,128)(2,1)} %param.12) | copy-start | bytes 49156
  101.4 9.1 %collective-permute-start.12 = (bf16[8,72,128]{2,1,0:T(8,128)(2,1)S(1)}, bf16[8,72,128]{2,1,0:T(8,128)(2,1)S(1)}, u32[]{:S(2)}, u32[]{:S(2)}) collective-permute-start(bf16[8,72,128]{2,1,0:T(8,128)(2,1)S(1)} %pad_maximum_fusion.9), channel_id=1, source_target_pairs={{0,4},{1,5},{2,6},{3,7},{4,8},{5,9},{6,10},{7,11},{8,12},{9,13},{1... | collective-permute-start | bytes 442376 | tf_op jit(solution)/shard_map/ppermute | solution.py:18
  105.4 16.8 %copy-start.8 = (f32[128,8]{0,1:T(8,128)S(1)}, f32[128,8]{0,1:T(8,128)}, u32[]{:S(2)}) copy-start(f32[128,8]{0,1:T(8,128)} %copy-done.7) | copy-start | bytes 12292
  105.4 11.5 %collective-permute-start.17 = (bf16[8,64,128]{2,1,0:T(8,128)(2,1)S(1)}, bf16[8,64,128]{2,1,0:T(8,128)(2,1)S(1)}, u32[]{:S(2)}, u32[]{:S(2)}) collective-permute-start(bf16[8,64,128]{2,1,0:T(8,128)(2,1)S(1)} %add_convert_fusion), channel_id=1, source_target_pairs={{1,0},{2,1},{3,2},{4,3},{5,4},{6,5},{7,6},{8,7},{9,8},{10,9},{11,1... | collective-permute-start | bytes 393224 | tf_op jit(solution)/shard_map/ppermute | solution.py:18
  106.9 7.8 %collective-permute-start.20 = (bf16[2,2,32,512]{3,2,1,0:T(8,128)(2,1)S(1)}, bf16[2,2,32,512]{3,2,1,0:T(8,128)(2,1)S(1)}, u32[]{:S(2)}, u32[]{:S(2)}) collective-permute-start(bf16[2,2,32,512]{3,2,1,0:T(8,128)(2,1)S(1)} %fusion.43), channel_id=1, source_target_pairs={{0,4},{1,5},{2,6},{3,7},{4,0},{5,1},{6,2},{7,3},{8,12},{9,13},{10,... | collective-permute-start | bytes 393224 | tf_op jit(solution)/shard_map/ppermute | solution.py:54
  110.6 11.5 %collective-permute-start.13 = (bf16[8,64,128]{2,1,0:T(8,128)(2,1)S(1)}, bf16[8,64,128]{2,1,0:T(8,128)(2,1)S(1)}, u32[]{:S(2)}, u32[]{:S(2)}) collective-permute-start(bf16[8,64,128]{2,1,0:T(8,128)(2,1)S(1)} %add_convert_fusion.3), channel_id=1, source_target_pairs={{0,1},{1,2},{2,3},{3,4},{4,5},{5,6},{6,7},{7,8},{8,9},{9,10},{10,1... | collective-permute-start | bytes 393224 | tf_op jit(solution)/shard_map/ppermute | solution.py:18
  114.8 5.9 %collective-permute-start.21 = (bf16[2,32,512]{2,1,0:T(8,128)(2,1)S(1)}, bf16[2,32,512]{2,1,0:T(8,128)(2,1)S(1)}, u32[]{:S(2)}, u32[]{:S(2)}) collective-permute-start(bf16[2,32,512]{2,1,0:T(8,128)(2,1)S(1)} %fusion.58), channel_id=1, source_target_pairs={{0,8},{1,9},{2,10},{3,11},{4,12},{5,13},{6,14},{7,15},{8,0},{9,1},... | collective-permute-start | bytes 196616 | tf_op jit(solution)/shard_map/ppermute | solution.py:54
  120.7 4.0 %collective-permute-start.22 = (bf16[32,512]{1,0:T(8,128)(2,1)S(1)}, bf16[32,512]{1,0:T(8,128)(2,1)S(1)}, u32[]{:S(2)}, u32[]{:S(2)}) collective-permute-start(bf16[32,512]{1,0:T(8,128)(2,1)S(1)} %fusion.59), channel_id=1, source_target_pairs={{0,16},{1,17},{2,18},{3,19},{4,20},{5,21},{6,22},{7,23},{8,24},{9,... | collective-permute-start | bytes 98312 | tf_op jit(solution)/shard_map/ppermute | solution.py:54
Sparse Core Ops, SparseCore 0:
  10.9 56.4 all-gather.1
